TPU v7x, 512 devices: a whole 4x4x16 slice. The times are simulated.
512 devices in a mesh: pix: 64 (over z, y_lo, core), tm: 8 (over y_hi, x).
Axes of the slice: x: 4, y: 4 (y_hi: 2, y_lo: 2; y = y_hi * 2 + y_lo), z: 16, core: 2. Of those that a mesh axis runs over, the one named last changes fastest.
Arguments:
- signal: bfloat16 [16384, 16, 256], P('pix', 'tm'), may hold values from -6 to 6
- lap_tiles: bfloat16 [256, 9, 64, 64], P('pix'), may hold values from -0.25 to 0.25
- neighbours: int32 [256, 9], replicated, may hold values from 0 to 255, as said below
- cheb_weight: bfloat16 [3, 256, 256], replicated, may hold values from -0.21875 to 0.21875
- norm_gain: float32 [256], replicated, may hold values from 0.25 to 1.75
- w_query: bfloat16 [256, 256], replicated, may hold values from -6.5 to 6.5
- w_key: bfloat16 [256, 256], replicated, may hold values from -0.375 to 0.375
- w_value: bfloat16 [256, 256], replicated, may hold values from -0.375 to 0.375
- w_out: bfloat16 [256, 256], replicated, may hold values from -0.375 to 0.375
Outputs:
- result: bfloat16 [16384, 16, 256], P('pix', 'tm')
Inputs may be any that keep to these rules, and one draw needn't show every extreme that they name: `neighbours`: row g lists blocks g - 2, g - 1, g, g + 1, g + 2 in its first five entries (g itself where one of them does not exist); each of the other four entries is one of those five.
All inputs are finite; a program needn't handle non-finite values.
Results may differ from a plain program's by a relative error of at most 0.017.
Values may be sent and summed in bfloat16 or wider, within the bound.
A program may use at most 64 MiB of HBM per device.

v0:
```python
from functools import partial
import math
import jax
import jax.numpy as jnp
from jax import lax
from jax.sharding import PartitionSpec as P

HEADS = 8
reach_blocks = 2


def with_halo(block, sides, width):
    for axis, dim in sides:
        count = lax.axis_size(axis)
        forward = [(i, i + 1) for i in range(count - 1)]
        backward = [(target, source) for source, target in forward]
        low = lax.ppermute(
            lax.slice_in_dim(block, block.shape[dim] - width, None, axis=dim), axis, forward
        )
        high = lax.ppermute(lax.slice_in_dim(block, 0, width, axis=dim), axis, backward)
        block = jnp.concatenate([low, block, high], axis=dim)
    return block


def apply_tiles(tile_blocks, source, sources_at):
    summed = None
    for slot in range(tile_blocks.shape[1]):
        chosen = jnp.take(source, sources_at[:, slot], axis=0, mode="clip")
        product = jnp.einsum(
            "gab,gbf->gaf", tile_blocks[:, slot], chosen, preferred_element_type=jnp.float32
        )
        summed = product if summed is None else summed + product
    return summed


def attend_group(grouped, norm_gain, w_query, w_key, w_value, w_out):
    block = grouped[0]
    count, times, channels = block.shape
    head_dim = channels // HEADS
    flat = block.reshape(count * times, channels).astype(jnp.float32)
    scaling = lax.rsqrt(jnp.mean(flat * flat, axis=1, keepdims=True) + 1e-06)
    normed = (flat * scaling * norm_gain[None, :]).astype(jnp.bfloat16)
    query = jnp.dot(normed, w_query, preferred_element_type=jnp.float32).astype(jnp.bfloat16)
    keys = jnp.dot(normed, w_key, preferred_element_type=jnp.float32).astype(jnp.bfloat16)
    values = jnp.dot(normed, w_value, preferred_element_type=jnp.float32).astype(jnp.bfloat16)
    query = query.reshape(count, times, HEADS, head_dim)
    keys = keys.reshape(count, times, HEADS, head_dim)
    values = values.reshape(count, times, HEADS, head_dim)
    scores = jnp.einsum(
        "pshd,pthd->phst", query, keys, preferred_element_type=jnp.float32
    ) / math.sqrt(head_dim)
    weights = jax.nn.softmax(scores, axis=-1).astype(jnp.bfloat16)
    attended = jnp.einsum(
        "phst,pthd->pshd", weights, values, preferred_element_type=jnp.float32
    ).astype(jnp.bfloat16)
    attended = attended.reshape(count * times, channels)
    output = flat + jnp.dot(attended, w_out, preferred_element_type=jnp.float32)
    return output.astype(jnp.bfloat16).reshape(1, count, times, channels)


def on_device(
    signal, lap_tiles, neighbours, cheb_weight, norm_gain, w_query, w_key, w_value, w_out
):
    pix_count, time_count, channels = signal.shape
    block_count = lap_tiles.shape[0]
    tile_size = lap_tiles.shape[2]
    features = time_count * channels
    blocks = signal.reshape(block_count, tile_size, features)
    first_block = lax.axis_index("pix") * block_count
    own_rows = lax.dynamic_slice_in_dim(neighbours, first_block, block_count, 0)
    sources_at = own_rows - first_block + reach_blocks
    extended = with_halo(blocks, (("pix", 0),), 2)
    first_order = apply_tiles(lap_tiles, extended, sources_at).astype(jnp.bfloat16)
    first_wide = with_halo(first_order, (("pix", 0),), 2)
    second_order = (
        2.0 * apply_tiles(lap_tiles, first_wide, sources_at) - blocks.astype(jnp.float32)
    ).astype(jnp.bfloat16)
    row_count = pix_count * time_count
    plain = signal.reshape(row_count, channels)
    stacked = jnp.concatenate(
        [
            plain,
            first_order.reshape(row_count, channels),
            second_order.reshape(row_count, channels),
        ],
        axis=1,
    )
    mixing = jnp.dot(
        stacked, cheb_weight.reshape(3 * channels, channels), preferred_element_type=jnp.float32
    )
    mixed = (plain.astype(jnp.float32) + jax.nn.silu(mixing)).astype(jnp.bfloat16)
    group_count = lax.axis_size("tm")
    grouped = mixed.reshape(group_count, pix_count // group_count, time_count, channels)
    attend_fn = partial(
        attend_group,
        norm_gain=norm_gain,
        w_query=w_query,
        w_key=w_key,
        w_value=w_value,
        w_out=w_out,
    )
    attended = attend_fn(lax.all_to_all(grouped, "tm", split_axis=0, concat_axis=2, tiled=True))
    returned = lax.all_to_all(attended, "tm", split_axis=2, concat_axis=0, tiled=True)
    return returned.reshape(pix_count, time_count, channels)


def solution(mesh):
    in_specs = (P("pix", "tm", None), P("pix", None, None, None), P(), P(), P(), P(), P(), P(), P())
    out_specs = P("pix", "tm", None)
    return jax.shard_map(
        on_device, mesh=mesh, in_specs=in_specs, out_specs=out_specs, check_vma=False
    )
```

profile of v0, /device:TPU:105, one launch (start us, length us, event | category | flops | bytes accessed | tf_op | source)
XLA Modules:
  0.0 98.8 jit_solution(3153955818766768114)
XLA Ops:
  1.3 5.2 %collective-permute-start = (bf16[2,64,512]{2,1,0:T(8,128)(2,1)S(1)}, bf16[2,64,512]{2,1,0:T(8,128)(2,1)S(1)}, u32[]{:S(2)}, u32[]{:S(2)}) collective-permute-start(bf16[2,64,512]{2,1,0:T(8,128)(2,1)S(1)} %slice.91), channel_id=1, source_target_pairs={{0,8},{8,16},{16,24},{24,32},{32,40},{40,48},{48,56},{56,64},{64,7... | collective-permute-start | bytes 393224 | tf_op jit(solution)/shard_map/ppermute | solution.py:17
  6.6 1.9 %collective-permute-start.1 = (bf16[2,64,512]{2,1,0:T(8,128)(2,1)S(1)}, bf16[2,64,512]{2,1,0:T(8,128)(2,1)S(1)}, u32[]{:S(2)}, u32[]{:S(2)}) collective-permute-start(bf16[2,64,512]{2,1,0:T(8,128)(2,1)S(1)} %slice.93), channel_id=1, source_target_pairs={{8,0},{16,8},{24,16},{32,24},{40,32},{48,40},{56,48},{64,56},{72,6... | collective-permute-start | bytes 393224 | tf_op jit(solution)/shard_map/ppermute | solution.py:20
  10.6 4.4 %collective-permute-done.1 = bf16[2,64,512]{2,1,0:T(8,128)(2,1)S(1)} collective-permute-done((bf16[2,64,512]{2,1,0:T(8,128)(2,1)S(1)}, bf16[2,64,512]{2,1,0:T(8,128)(2,1)S(1)}, u32[]{:S(2)}, u32[]{:S(2)}) %collective-permute-start.1) | collective-permute-done | bytes 131104 | tf_op jit(solution)/shard_map/ppermute | solution.py:20
  16.6 1.3 %gather_fusion.5 = bf16[4,64,512]{2,1,0:T(8,128)(2,1)} fusion(bf16[8,64,512]{2,1,0:T(8,128)(2,1)S(1)} %constant_dynamic-update-slice_fusion, s32[1024]{0:T(1024)S(1)} %get-tuple-element.23), kind=kCustom, calls=%fused_computation.5 | custom fusion | bytes 524304 | tf_op jit(solution)/shard_map/jit(_take)/gather | solution.py:28
  19.0 1.3 %gather_fusion.4 = bf16[4,64,512]{2,1,0:T(8,128)(2,1)} fusion(bf16[8,64,512]{2,1,0:T(8,128)(2,1)S(1)} %constant_dynamic-update-slice_fusion, s32[1024]{0:T(1024)S(1)} %get-tuple-element.24), kind=kCustom, calls=%fused_computation.4 | custom fusion | bytes 524304 | tf_op jit(solution)/shard_map/jit(_take)/gather | solution.py:28
  20.3 1.9 %fusion.55 = f32[4,512,64]{1,2,0:T(8,128)} fusion(bf16[4,64,512]{2,1,0:T(8,128)(2,1)} %gather_fusion.4, bf16[4,9,64,64]{3,2,1,0:T(8,128)(2,1)S(1)} %copy-done.2), kind=kOutput, calls=%fused_computation.86 | convolution fusion | flops 16777216 | bytes 851968 | tf_op jit(solution)/shard_map/gab,gbf->gaf/dot_general | solution.py:29
  22.3 1.3 %gather_fusion.3 = bf16[4,64,512]{2,1,0:T(8,128)(2,1)} fusion(bf16[8,64,512]{2,1,0:T(8,128)(2,1)S(1)} %constant_dynamic-update-slice_fusion, s32[1024]{0:T(1024)S(1)} %get-tuple-element.25), kind=kCustom, calls=%fused_computation.3 | custom fusion | bytes 524304 | tf_op jit(solution)/shard_map/jit(_take)/gather | solution.py:28
  23.5 2.0 %fusion.59 = f32[4,512,64]{1,2,0:T(8,128)} fusion(bf16[4,64,512]{2,1,0:T(8,128)(2,1)} %gather_fusion.3, bf16[4,9,64,64]{3,2,1,0:T(8,128)(2,1)S(1)} %copy-done.2), kind=kOutput, calls=%fused_computation.90 | convolution fusion | flops 16777216 | bytes 851968 | tf_op jit(solution)/shard_map/gab,gbf->gaf/dot_general | solution.py:29
  25.5 1.3 %gather_fusion.2 = bf16[4,64,512]{2,1,0:T(8,128)(2,1)} fusion(bf16[8,64,512]{2,1,0:T(8,128)(2,1)S(1)} %constant_dynamic-update-slice_fusion, s32[1024]{0:T(1024)S(1)} %get-tuple-element.26), kind=kCustom, calls=%fused_computation.2 | custom fusion | bytes 524304 | tf_op jit(solution)/shard_map/jit(_take)/gather | solution.py:28
  26.8 2.0 %fusion.63 = f32[4,512,64]{1,2,0:T(8,128)} fusion(bf16[4,64,512]{2,1,0:T(8,128)(2,1)} %gather_fusion.2, bf16[4,9,64,64]{3,2,1,0:T(8,128)(2,1)S(1)} %copy-done.2), kind=kOutput, calls=%fused_computation.94 | convolution fusion | flops 16777216 | bytes 851968 | tf_op jit(solution)/shard_map/gab,gbf->gaf/dot_general | solution.py:29
  30.0 2.0 %fusion.67 = f32[4,512,64]{1,2,0:T(8,128)} fusion(bf16[4,64,512]{2,1,0:T(8,128)(2,1)} %gather_fusion.1, bf16[4,9,64,64]{3,2,1,0:T(8,128)(2,1)S(1)} %copy-done.2), kind=kOutput, calls=%fused_computation.98 | convolution fusion | flops 16777216 | bytes 851968 | tf_op jit(solution)/shard_map/gab,gbf->gaf/dot_general | solution.py:29
  33.2 2.0 %fusion.39 = f32[4,512,64]{1,2,0:T(8,128)} fusion(bf16[4,64,512]{2,1,0:T(8,128)(2,1)} %gather_fusion.8, bf16[4,9,64,64]{3,2,1,0:T(8,128)(2,1)S(1)} %copy-done.2), kind=kOutput, calls=%fused_computation.70 | convolution fusion | flops 16777216 | bytes 851968 | tf_op jit(solution)/shard_map/gab,gbf->gaf/dot_general | solution.py:29
  36.5 2.1 %fusion.23 = bf16[4,64,512]{2,1,0:T(8,128)(2,1)S(1)} fusion(f32[4,512,64]{1,2,0:T(8,128)} %fusion.39, f32[4,512,64]{1,2,0:T(8,128)S(1)} %fusion.43, f32[4,512,64]{1,2,0:T(8,128)S(1)} %fusion.47, f32[4,512,64]{1,2,0:T(8,128)S(1)} %fusion.51, f32[4,512,64]{1,2,0:T(8,128)} %fusion.55, f32[4,512,64]{1,2,0:T(8,128)} %fusion.59, f32[4,512,64]{1,2,0:T(8,128)} %fusion.63, ...), kind=kOutput, calls=%fused_computation.51 | convolution fusion | flops 17956864 | bytes 4784128 | tf_op jit(solution)/shard_map/gab,gbf->gaf/dot_general | solution.py:29
  38.6 1.9 %collective-permute-start.2 = (bf16[2,64,512]{2,1,0:T(8,128)(2,1)S(1)}, bf16[2,64,512]{2,1,0:T(8,128)(2,1)S(1)}, u32[]{:S(2)}, u32[]{:S(2)}) collective-permute-start(bf16[2,64,512]{2,1,0:T(8,128)(2,1)S(1)} %get-tuple-element.5), channel_id=1, source_target_pairs={{0,8},{8,16},{16,24},{24,32},{32,40},{40,48},{48,56},{56,64},{64,7... | collective-permute-start | bytes 393224 | tf_op jit(solution)/shard_map/ppermute | solution.py:17
  40.5 2.4 %collective-permute-start.3 = (bf16[2,64,512]{2,1,0:T(8,128)(2,1)S(1)}, bf16[2,64,512]{2,1,0:T(8,128)(2,1)S(1)}, u32[]{:S(2)}, u32[]{:S(2)}) collective-permute-start(bf16[2,64,512]{2,1,0:T(8,128)(2,1)S(1)} %get-tuple-element.6), channel_id=1, source_target_pairs={{8,0},{16,8},{24,16},{32,24},{40,32},{48,40},{56,48},{64,56},{72,6... | collective-permute-start | bytes 393224 | tf_op jit(solution)/shard_map/ppermute | solution.py:20
  44.5 4.4 %collective-permute-done.3 = bf16[2,64,512]{2,1,0:T(8,128)(2,1)S(1)} collective-permute-done((bf16[2,64,512]{2,1,0:T(8,128)(2,1)S(1)}, bf16[2,64,512]{2,1,0:T(8,128)(2,1)S(1)}, u32[]{:S(2)}, u32[]{:S(2)}) %collective-permute-start.3) | collective-permute-done | bytes 131104 | tf_op jit(solution)/shard_map/ppermute | solution.py:20
  51.9 1.3 %gather_fusion.11 = bf16[4,64,512]{2,1,0:T(8,128)(2,1)} fusion(bf16[8,64,512]{2,1,0:T(8,128)(2,1)S(1)} %pad_maximum_fusion, s32[1024]{0:T(1024)S(1)} %get-tuple-element.26), kind=kCustom, calls=%fused_computation.11 | custom fusion | bytes 524304 | tf_op jit(solution)/shard_map/jit(_take)/gather | solution.py:28
  53.1 1.3 %gather_fusion.10 = bf16[4,64,512]{2,1,0:T(8,128)(2,1)} fusion(bf16[8,64,512]{2,1,0:T(8,128)(2,1)S(1)} %pad_maximum_fusion, s32[1024]{0:T(1024)S(1)} %get-tuple-element.27), kind=kCustom, calls=%fused_computation.10 | custom fusion | bytes 524304 | tf_op jit(solution)/shard_map/jit(_take)/gather | solution.py:28
  59.5 13.5 %all_to_all.24 = bf16[8,32,2,256]{3,2,1,0:T(2,128)(2,1)S(1)} all-to-all(bf16[8,32,2,256]{3,2,1,0:T(2,128)(2,1)S(1)} %reshape.71), channel_id=1, replica_groups=mesh['pix'=64,'tm'=8] {'tm'}, dimensions={0} | all-to-all | bytes 524288 | tf_op jit(solution)/shard_map/all_to_all | solution.py:102
  76.4 1.7 %reshape.74 = bf16[32,16,8,32]{3,2,1,0:T(8,128)(2,1)S(1)} reshape(bf16[512,256]{1,0:T(8,128)(2,1)} %convolution_convert_fusion.1) | data formatting | bytes 524288 | tf_op jit(solution)/shard_map/reshape | solution.py:47
  79.0 2.4 %reshape.72 = bf16[32,16,8,32]{3,2,1,0:T(8,128)(2,1)} reshape(bf16[512,256]{1,0:T(8,128)(2,1)} %convolution_convert_fusion.3) | data formatting | bytes 524288 | tf_op jit(solution)/shard_map/reshape | solution.py:48
  81.4 2.6 %fusion.107 = (f32[32,8,16]{2,1,0:T(8,128)S(1)}, f32[32,8,16,16]{2,3,1,0:T(8,128)}) fusion(bf16[32,16,8,32]{3,2,1,0:T(8,128)(2,1)S(1)} %reshape.74, bf16[32,16,8,32]{3,2,1,0:T(8,128)(2,1)S(1)} %reshape.73), kind=kOutput, calls=%fused_computation.149 | convolution fusion | flops 4390927 | bytes 802816 | tf_op jit(solution)/shard_map/sub | solution.py:52
  84.0 2.5 %fusion.2 = bf16[32,16,8,32]{3,1,2,0:T(8,128)(2,1)S(1)} fusion(f32[32,8,16,16]{2,3,1,0:T(8,128)} %get-tuple-element.19, bf16[32,16,8,32]{3,2,1,0:T(8,128)(2,1)} %reshape.72, f32[32,8,16]{2,1,0:T(8,128)S(1)} %get-tuple-element.18), kind=kOutput, calls=%fused_computation.24 | convolution fusion | flops 4456448 | bytes 802816 | tf_op jit(solution)/shard_map/phst,pthd->pshd/dot_general | solution.py:53
  87.8 10.1 %all_to_all.25 = bf16[1,32,16,256]{3,1,0,2:T(8,128)(2,1)S(1)} all-to-all(bf16[1,32,16,256]{3,1,0,2:T(8,128)(2,1)S(1)} %copy.76), channel_id=1, replica_groups=mesh['pix'=64,'tm'=8] {'tm'}, dimensions={2} | all-to-all | bytes 524288 | tf_op jit(solution)/shard_map/all_to_all | solution.py:103
  (91 shorter events, 25.8 us)
Async XLA Ops:
  0.0 58.4 %copy-start = (bf16[3,256,256]{2,1,0:T(8,128)(2,1)S(1)}, bf16[3,256,256]{2,1,0:T(8,128)(2,1)}, u32[]{:S(2)}) copy-start(bf16[3,256,256]{2,1,0:T(8,128)(2,1)} %param.12) | copy-start | bytes 1179652
  0.0 16.2 %copy-start.2 = (bf16[4,9,64,64]{3,2,1,0:T(8,128)(2,1)S(1)}, bf16[4,9,64,64]{3,2,1,0:T(8,128)(2,1)}, u32[]{:S(2)}) copy-start(bf16[4,9,64,64]{3,2,1,0:T(8,128)(2,1)} %param.10) | copy-start | bytes 884740
  1.3 9.2 %collective-permute-start = (bf16[2,64,512]{2,1,0:T(8,128)(2,1)S(1)}, bf16[2,64,512]{2,1,0:T(8,128)(2,1)S(1)}, u32[]{:S(2)}, u32[]{:S(2)}) collective-permute-start(bf16[2,64,512]{2,1,0:T(8,128)(2,1)S(1)} %slice.91), channel_id=1, source_target_pairs={{0,8},{8,16},{16,24},{24,32},{32,40},{40,48},{48,56},{56,64},{64,7... | collective-permute-start | bytes 393224 | tf_op jit(solution)/shard_map/ppermute | solution.py:17
  6.6 8.4 %collective-permute-start.1 = (bf16[2,64,512]{2,1,0:T(8,128)(2,1)S(1)}, bf16[2,64,512]{2,1,0:T(8,128)(2,1)S(1)}, u32[]{:S(2)}, u32[]{:S(2)}) collective-permute-start(bf16[2,64,512]{2,1,0:T(8,128)(2,1)S(1)} %slice.93), channel_id=1, source_target_pairs={{8,0},{16,8},{24,16},{32,24},{40,32},{48,40},{56,48},{64,56},{72,6... | collective-permute-start | bytes 393224 | tf_op jit(solution)/shard_map/ppermute | solution.py:20
  36.5 6.5 %copy-start.1 = (bf16[256,2,256]{2,1,0:T(2,128)(2,1)S(1)}, bf16[256,2,256]{2,1,0:T(2,128)(2,1)}, u32[]{:S(2)}) copy-start(bf16[256,2,256]{2,1,0:T(2,128)(2,1)} %param.9) | copy-start | bytes 786436
  38.6 5.9 %collective-permute-start.2 = (bf16[2,64,512]{2,1,0:T(8,128)(2,1)S(1)}, bf16[2,64,512]{2,1,0:T(8,128)(2,1)S(1)}, u32[]{:S(2)}, u32[]{:S(2)}) collective-permute-start(bf16[2,64,512]{2,1,0:T(8,128)(2,1)S(1)} %get-tuple-element.5), channel_id=1, source_target_pairs={{0,8},{8,16},{16,24},{24,32},{32,40},{40,48},{48,56},{56,64},{64,7... | collective-permute-start | bytes 393224 | tf_op jit(solution)/shard_map/ppermute | solution.py:17
  40.5 8.4 %collective-permute-start.3 = (bf16[2,64,512]{2,1,0:T(8,128)(2,1)S(1)}, bf16[2,64,512]{2,1,0:T(8,128)(2,1)S(1)}, u32[]{:S(2)}, u32[]{:S(2)}) collective-permute-start(bf16[2,64,512]{2,1,0:T(8,128)(2,1)S(1)} %get-tuple-element.6), channel_id=1, source_target_pairs={{8,0},{16,8},{24,16},{32,24},{40,32},{48,40},{56,48},{64,56},{72,6... | collective-permute-start | bytes 393224 | tf_op jit(solution)/shard_map/ppermute | solution.py:20
  56.2 1.1 %copy-start.3 = (bf16[4,64,512]{2,1,0:T(8,128)(2,1)S(1)}, bf16[4,64,512]{2,1,0:T(8,128)(2,1)}, u32[]{:S(2)}) copy-start(bf16[4,64,512]{2,1,0:T(8,128)(2,1)} %gather_fusion.11) | copy-start | bytes 786436
  56.4 1.1 %copy-start.4 = (bf16[4,64,512]{2,1,0:T(8,128)(2,1)S(1)}, bf16[4,64,512]{2,1,0:T(8,128)(2,1)}, u32[]{:S(2)}) copy-start(bf16[4,64,512]{2,1,0:T(8,128)(2,1)} %gather_fusion.10) | copy-start | bytes 786436
  56.7 1.1 %copy-start.5 = (bf16[4,64,512]{2,1,0:T(8,128)(2,1)S(1)}, bf16[4,64,512]{2,1,0:T(8,128)(2,1)}, u32[]{:S(2)}) copy-start(bf16[4,64,512]{2,1,0:T(8,128)(2,1)} %gather_fusion.17) | copy-start | bytes 786436
  57.9 1.0 copy-start.6
  57.9 1.0 %copy-start.7 = (bf16[512,256]{1,0:T(8,128)(2,1)S(1)}, bf16[512,256]{1,0:T(8,128)(2,1)}, u32[]{:S(2)}) copy-start(bf16[512,256]{1,0:T(8,128)(2,1)} %reshape.68) | copy-start | bytes 786436
  59.5 15.1 %copy-start.12 = (f32[256]{0:T(256)S(1)}, f32[256]{0:T(256)}, u32[]{:S(2)}) copy-start(f32[256]{0:T(256)} %param.13) | copy-start | bytes 3076
  73.0 1.8 %copy-start.8 = (bf16[256,256]{1,0:T(8,128)(2,1)S(1)}, bf16[256,256]{1,0:T(8,128)(2,1)}, u32[]{:S(2)}) copy-start(bf16[256,256]{1,0:T(8,128)(2,1)} %param.14) | copy-start | bytes 393220
  73.4 2.0 %copy-start.9 = (bf16[256,256]{1,0:T(8,128)(2,1)S(1)}, bf16[256,256]{1,0:T(8,128)(2,1)}, u32[]{:S(2)}) copy-start(bf16[256,256]{1,0:T(8,128)(2,1)} %param.15) | copy-start | bytes 393220
  74.8 3.3 %copy-start.10 = (bf16[256,256]{1,0:T(8,128)(2,1)S(1)}, bf16[256,256]{1,0:T(8,128)(2,1)}, u32[]{:S(2)}) copy-start(bf16[256,256]{1,0:T(8,128)(2,1)} %param.16) | copy-start | bytes 393220
  86.5 1.0 %copy-start.11 = (bf16[256,256]{1,0:T(8,128)(2,1)S(1)}, bf16[256,256]{1,0:T(8,128)(2,1)}, u32[]{:S(2)}) copy-start(bf16[256,256]{1,0:T(8,128)(2,1)} %param.17) | copy-start | bytes 393220
where the time goes:
time: 99.5 us; the launch traced here: 98.8 us
  local copies, waits for them, and re-layouts  29.7 us (30%)
  blocking collectives  23.5 us (24%)
  matrix products  23.2 us (23%)
  starting transfers between devices  11.5 us (12%)
  waiting for transfers between devices  8.82 us (9%)
  other arithmetic  1.55 us (2%)
    gather x18, local copies, waits for them, and re-layouts, apply_tiles(): chosen = jnp.take(source, sources_at[:, slot], axis=0, mode='clip')  17.2 us
    dot_general x18, matrix products, apply_tiles(): jnp.einsum('gab,gbf->gaf', tile_blocks[:, slot], chosen, preferred_elemen...  15.4 us
    all_to_all x1, blocking collectives, on_device(): lax.all_to_all(grouped, 'tm', split_axis=0, concat_axis=2, tiled=True)  13.5 us
    all_to_all x1, blocking collectives, on_device(): lax.all_to_all(attended, 'tm', split_axis=2, concat_axis=0, tiled=True)  10.1 us
    ppermute x2, waiting for transfers between devices, with_halo(): lax.ppermute(lax.slice_in_dim(block, 0, width, axis=dim), axis, backward)  8.82 us
    ppermute x2, starting transfers between devices, with_halo(): lax.ppermute(lax.slice_in_dim(block, block.shape[dim] - width, None, axis...  7.12 us
    ppermute x2, starting transfers between devices, with_halo(): lax.ppermute(lax.slice_in_dim(block, 0, width, axis=dim), axis, backward)  4.33 us
    sub x1, matrix products, attend_group(): weights = jax.nn.softmax(scores, axis=-1).astype(jnp.bfloat16)  2.57 us
  transfers between devices with their start and end apart: 4, of which 2 were waited for; matrix products, arithmetic and copies ran while one was open for 4% of the time, Pallas kernels for 0%

commit v1 on v0

--- a/solution.py
+++ b/solution.py
@@ -100,7 +100,10 @@
         w_out=w_out,
     )
     attended = attend_fn(lax.all_to_all(grouped, "tm", split_axis=0, concat_axis=2, tiled=True))
-    returned = lax.all_to_all(attended, "tm", split_axis=2, concat_axis=0, tiled=True)
+    returned = jnp.concatenate(
+        lax.all_to_all(jnp.stack(jnp.split(attended, lax.axis_size("tm"), axis=2)), "tm", 0, 0),
+        axis=0,
+    )
     return returned.reshape(pix_count, time_count, channels)
 
 

time: 99.5 us -> 96.7 us (0.972)
  local copies, waits for them, and re-layouts: 29.7 us -> 27.5 us
    reshape x1, local copies, waits for them, and re-layouts: 1.66 us -> 0.44 us  [attend_group(): keys = keys.reshape(count, times, HEADS, head_dim)]
    reshape x1, local copies, waits for them, and re-layouts: 2.42 us -> 1.41 us  [attend_group(): values = values.reshape(count, times, HEADS, head_dim)]
where the time goes in v1:
time: 96.7 us; the launch traced here: 96.1 us
  local copies, waits for them, and re-layouts  27.5 us (28%)
  blocking collectives  23.5 us (24%)
  matrix products  22.7 us (23%)
  starting transfers between devices  11.5 us (12%)
  waiting for transfers between devices  8.81 us (9%)
  other arithmetic  1.55 us (2%)
    gather x18, local copies, waits for them, and re-layouts, apply_tiles(): chosen = jnp.take(source, sources_at[:, slot], axis=0, mode='clip')  17.2 us
    dot_general x18, matrix products, apply_tiles(): jnp.einsum('gab,gbf->gaf', tile_blocks[:, slot], chosen, preferred_elemen...  15.4 us
    all_to_all x1, blocking collectives, on_device(): lax.all_to_all(grouped, 'tm', split_axis=0, concat_axis=2, tiled=True)  13.5 us
    all_to_all x1, blocking collectives, on_device(): lax.all_to_all(jnp.stack(jnp.split(attended, lax.axis_size('tm'), axis=2)...  10.1 us
    ppermute x2, waiting for transfers between devices, with_halo(): lax.ppermute(lax.slice_in_dim(block, 0, width, axis=dim), axis, backward)  8.8 us
    ppermute x2, starting transfers between devices, with_halo(): lax.ppermute(lax.slice_in_dim(block, block.shape[dim] - width, None, axis...  7.12 us
    ppermute x2, starting transfers between devices, with_halo(): lax.ppermute(lax.slice_in_dim(block, 0, width, axis=dim), axis, backward)  4.33 us
    sub x1, matrix products, attend_group(): weights = jax.nn.softmax(scores, axis=-1).astype(jnp.bfloat16)  2.58 us
  transfers between devices with their start and end apart: 4, of which 2 were waited for; matrix products, arithmetic and copies ran while one was open for 4% of the time, Pallas kernels for 0%

profile of v1, /device:TPU:105, one launch (start us, length us, event | category | flops | bytes accessed | tf_op | source)
XLA Modules:
  0.0 96.1 jit_solution(14192504766297645534)
XLA Ops:
  1.3 5.2 %collective-permute-start = (bf16[2,64,512]{2,1,0:T(8,128)(2,1)S(1)}, bf16[2,64,512]{2,1,0:T(8,128)(2,1)S(1)}, u32[]{:S(2)}, u32[]{:S(2)}) collective-permute-start(bf16[2,64,512]{2,1,0:T(8,128)(2,1)S(1)} %slice.91), channel_id=1, source_target_pairs={{0,8},{8,16},{16,24},{24,32},{32,40},{40,48},{48,56},{56,64},{64,7... | collective-permute-start | bytes 393224 | tf_op jit(solution)/shard_map/ppermute | solution.py:17
  6.6 1.9 %collective-permute-start.1 = (bf16[2,64,512]{2,1,0:T(8,128)(2,1)S(1)}, bf16[2,64,512]{2,1,0:T(8,128)(2,1)S(1)}, u32[]{:S(2)}, u32[]{:S(2)}) collective-permute-start(bf16[2,64,512]{2,1,0:T(8,128)(2,1)S(1)} %slice.93), channel_id=1, source_target_pairs={{8,0},{16,8},{24,16},{32,24},{40,32},{48,40},{56,48},{64,56},{72,6... | collective-permute-start | bytes 393224 | tf_op jit(solution)/shard_map/ppermute | solution.py:20
  10.6 4.4 %collective-permute-done.1 = bf16[2,64,512]{2,1,0:T(8,128)(2,1)S(1)} collective-permute-done((bf16[2,64,512]{2,1,0:T(8,128)(2,1)S(1)}, bf16[2,64,512]{2,1,0:T(8,128)(2,1)S(1)}, u32[]{:S(2)}, u32[]{:S(2)}) %collective-permute-start.1) | collective-permute-done | bytes 131104 | tf_op jit(solution)/shard_map/ppermute | solution.py:20
  16.6 1.3 %gather_fusion.5 = bf16[4,64,512]{2,1,0:T(8,128)(2,1)} fusion(bf16[8,64,512]{2,1,0:T(8,128)(2,1)S(1)} %constant_dynamic-update-slice_fusion, s32[1024]{0:T(1024)S(1)} %get-tuple-element.23), kind=kCustom, calls=%fused_computation.5 | custom fusion | bytes 524304 | tf_op jit(solution)/shard_map/jit(_take)/gather | solution.py:28
  19.0 1.3 %gather_fusion.4 = bf16[4,64,512]{2,1,0:T(8,128)(2,1)} fusion(bf16[8,64,512]{2,1,0:T(8,128)(2,1)S(1)} %constant_dynamic-update-slice_fusion, s32[1024]{0:T(1024)S(1)} %get-tuple-element.24), kind=kCustom, calls=%fused_computation.4 | custom fusion | bytes 524304 | tf_op jit(solution)/shard_map/jit(_take)/gather | solution.py:28
  20.3 1.9 %fusion.55 = f32[4,512,64]{1,2,0:T(8,128)} fusion(bf16[4,64,512]{2,1,0:T(8,128)(2,1)} %gather_fusion.4, bf16[4,9,64,64]{3,2,1,0:T(8,128)(2,1)S(1)} %copy-done.2), kind=kOutput, calls=%fused_computation.86 | convolution fusion | flops 16777216 | bytes 851968 | tf_op jit(solution)/shard_map/gab,gbf->gaf/dot_general | solution.py:29
  22.3 1.3 %gather_fusion.3 = bf16[4,64,512]{2,1,0:T(8,128)(2,1)} fusion(bf16[8,64,512]{2,1,0:T(8,128)(2,1)S(1)} %constant_dynamic-update-slice_fusion, s32[1024]{0:T(1024)S(1)} %get-tuple-element.25), kind=kCustom, calls=%fused_computation.3 | custom fusion | bytes 524304 | tf_op jit(solution)/shard_map/jit(_take)/gather | solution.py:28
  23.5 2.0 %fusion.59 = f32[4,512,64]{1,2,0:T(8,128)} fusion(bf16[4,64,512]{2,1,0:T(8,128)(2,1)} %gather_fusion.3, bf16[4,9,64,64]{3,2,1,0:T(8,128)(2,1)S(1)} %copy-done.2), kind=kOutput, calls=%fused_computation.90 | convolution fusion | flops 16777216 | bytes 851968 | tf_op jit(solution)/shard_map/gab,gbf->gaf/dot_general | solution.py:29
  25.5 1.3 %gather_fusion.2 = bf16[4,64,512]{2,1,0:T(8,128)(2,1)} fusion(bf16[8,64,512]{2,1,0:T(8,128)(2,1)S(1)} %constant_dynamic-update-slice_fusion, s32[1024]{0:T(1024)S(1)} %get-tuple-element.26), kind=kCustom, calls=%fused_computation.2 | custom fusion | bytes 524304 | tf_op jit(solution)/shard_map/jit(_take)/gather | solution.py:28
  26.8 2.0 %fusion.63 = f32[4,512,64]{1,2,0:T(8,128)} fusion(bf16[4,64,512]{2,1,0:T(8,128)(2,1)} %gather_fusion.2, bf16[4,9,64,64]{3,2,1,0:T(8,128)(2,1)S(1)} %copy-done.2), kind=kOutput, calls=%fused_computation.94 | convolution fusion | flops 16777216 | bytes 851968 | tf_op jit(solution)/shard_map/gab,gbf->gaf/dot_general | solution.py:29
  28.7 1.3 %gather_fusion.1 = bf16[4,64,512]{2,1,0:T(8,128)(2,1)} fusion(bf16[8,64,512]{2,1,0:T(8,128)(2,1)S(1)} %constant_dynamic-update-slice_fusion, s32[1024]{0:T(1024)S(1)} %get-tuple-element.27), kind=kCustom, calls=%fused_computation.1 | custom fusion | bytes 524304 | tf_op jit(solution)/shard_map/jit(_take)/gather | solution.py:28
  30.0 2.0 %fusion.67 = f32[4,512,64]{1,2,0:T(8,128)} fusion(bf16[4,64,512]{2,1,0:T(8,128)(2,1)} %gather_fusion.1, bf16[4,9,64,64]{3,2,1,0:T(8,128)(2,1)S(1)} %copy-done.2), kind=kOutput, calls=%fused_computation.98 | convolution fusion | flops 16777216 | bytes 851968 | tf_op jit(solution)/shard_map/gab,gbf->gaf/dot_general | solution.py:29
  33.2 1.9 %fusion.39 = f32[4,512,64]{1,2,0:T(8,128)} fusion(bf16[4,64,512]{2,1,0:T(8,128)(2,1)} %gather_fusion.8, bf16[4,9,64,64]{3,2,1,0:T(8,128)(2,1)S(1)} %copy-done.2), kind=kOutput, calls=%fused_computation.70 | convolution fusion | flops 16777216 | bytes 851968 | tf_op jit(solution)/shard_map/gab,gbf->gaf/dot_general | solution.py:29
  36.4 2.1 %fusion.23 = bf16[4,64,512]{2,1,0:T(8,128)(2,1)S(1)} fusion(f32[4,512,64]{1,2,0:T(8,128)} %fusion.39, f32[4,512,64]{1,2,0:T(8,128)S(1)} %fusion.43, f32[4,512,64]{1,2,0:T(8,128)S(1)} %fusion.47, f32[4,512,64]{1,2,0:T(8,128)S(1)} %fusion.51, f32[4,512,64]{1,2,0:T(8,128)} %fusion.55, f32[4,512,64]{1,2,0:T(8,128)} %fusion.59, f32[4,512,64]{1,2,0:T(8,128)} %fusion.63, ...), kind=kOutput, calls=%fused_computation.51 | convolution fusion | flops 17956864 | bytes 4784128 | tf_op jit(solution)/shard_map/gab,gbf->gaf/dot_general | solution.py:29
  38.6 1.9 %collective-permute-start.2 = (bf16[2,64,512]{2,1,0:T(8,128)(2,1)S(1)}, bf16[2,64,512]{2,1,0:T(8,128)(2,1)S(1)}, u32[]{:S(2)}, u32[]{:S(2)}) collective-permute-start(bf16[2,64,512]{2,1,0:T(8,128)(2,1)S(1)} %get-tuple-element.5), channel_id=1, source_target_pairs={{0,8},{8,16},{16,24},{24,32},{32,40},{40,48},{48,56},{56,64},{64,7... | collective-permute-start | bytes 393224 | tf_op jit(solution)/shard_map/ppermute | solution.py:17
  40.5 2.4 %collective-permute-start.3 = (bf16[2,64,512]{2,1,0:T(8,128)(2,1)S(1)}, bf16[2,64,512]{2,1,0:T(8,128)(2,1)S(1)}, u32[]{:S(2)}, u32[]{:S(2)}) collective-permute-start(bf16[2,64,512]{2,1,0:T(8,128)(2,1)S(1)} %get-tuple-element.6), channel_id=1, source_target_pairs={{8,0},{16,8},{24,16},{32,24},{40,32},{48,40},{56,48},{64,56},{72,6... | collective-permute-start | bytes 393224 | tf_op jit(solution)/shard_map/ppermute | solution.py:20
  44.5 4.4 %collective-permute-done.3 = bf16[2,64,512]{2,1,0:T(8,128)(2,1)S(1)} collective-permute-done((bf16[2,64,512]{2,1,0:T(8,128)(2,1)S(1)}, bf16[2,64,512]{2,1,0:T(8,128)(2,1)S(1)}, u32[]{:S(2)}, u32[]{:S(2)}) %collective-permute-start.3) | collective-permute-done | bytes 131104 | tf_op jit(solution)/shard_map/ppermute | solution.py:20
  51.8 1.3 %gather_fusion.11 = bf16[4,64,512]{2,1,0:T(8,128)(2,1)} fusion(bf16[8,64,512]{2,1,0:T(8,128)(2,1)S(1)} %pad_maximum_fusion, s32[1024]{0:T(1024)S(1)} %get-tuple-element.26), kind=kCustom, calls=%fused_computation.11 | custom fusion | bytes 524304 | tf_op jit(solution)/shard_map/jit(_take)/gather | solution.py:28
  53.1 1.3 %gather_fusion.10 = bf16[4,64,512]{2,1,0:T(8,128)(2,1)} fusion(bf16[8,64,512]{2,1,0:T(8,128)(2,1)S(1)} %pad_maximum_fusion, s32[1024]{0:T(1024)S(1)} %get-tuple-element.27), kind=kCustom, calls=%fused_computation.10 | custom fusion | bytes 524304 | tf_op jit(solution)/shard_map/jit(_take)/gather | solution.py:28
  59.5 13.5 %all_to_all.14 = bf16[8,32,2,256]{3,2,1,0:T(2,128)(2,1)S(1)} all-to-all(bf16[8,32,2,256]{3,2,1,0:T(2,128)(2,1)S(1)} %reshape.67), channel_id=1, replica_groups=mesh['pix'=64,'tm'=8] {'tm'}, dimensions={0} | all-to-all | bytes 524288 | tf_op jit(solution)/shard_map/all_to_all | solution.py:102
  77.3 1.4 %reshape.68 = bf16[32,16,8,32]{3,2,1,0:T(8,128)(2,1)} reshape(bf16[512,256]{1,0:T(8,128)(2,1)S(1)} %convolution_convert_fusion.3) | data formatting | bytes 524288 | tf_op jit(solution)/shard_map/reshape | solution.py:48
  78.7 2.6 %fusion.115 = (f32[32,8,16]{2,1,0:T(8,128)S(1)}, f32[32,8,16,16]{2,3,1,0:T(8,128)}) fusion(bf16[32,16,8,32]{3,2,1,0:T(8,128)(2,1)S(1)} %reshape.70, bf16[32,16,8,32]{3,2,1,0:T(8,128)(2,1)S(1)} %reshape.69), kind=kOutput, calls=%fused_computation.165 | convolution fusion | flops 4390927 | bytes 802816 | tf_op jit(solution)/shard_map/sub | solution.py:52
  81.2 2.5 %fusion.2 = bf16[32,16,8,32]{3,1,2,0:T(8,128)(2,1)S(1)} fusion(f32[32,8,16,16]{2,3,1,0:T(8,128)} %get-tuple-element.19, bf16[32,16,8,32]{3,2,1,0:T(8,128)(2,1)} %reshape.68, f32[32,8,16]{2,1,0:T(8,128)S(1)} %get-tuple-element.18), kind=kOutput, calls=%fused_computation.24 | convolution fusion | flops 4456448 | bytes 802816 | tf_op jit(solution)/shard_map/phst,pthd->pshd/dot_general | solution.py:53
  85.3 10.1 %all_to_all.15 = bf16[8,1,32,2,256]{4,3,2,1,0:T(2,128)(2,1)S(1)} all-to-all(bf16[8,1,32,2,256]{4,3,2,1,0:T(2,128)(2,1)S(1)} %fusion.91), channel_id=1, replica_groups=mesh['pix'=64,'tm'=8] {'tm'}, dimensions={0} | all-to-all | bytes 524288 | tf_op jit(solution)/shard_map/all_to_all | solution.py:104
  (96 shorter events, 24.5 us)
Async XLA Ops:
  0.0 58.4 %copy-start = (bf16[3,256,256]{2,1,0:T(8,128)(2,1)S(1)}, bf16[3,256,256]{2,1,0:T(8,128)(2,1)}, u32[]{:S(2)}) copy-start(bf16[3,256,256]{2,1,0:T(8,128)(2,1)} %param.12) | copy-start | bytes 1179652
  0.0 16.2 %copy-start.2 = (bf16[4,9,64,64]{3,2,1,0:T(8,128)(2,1)S(1)}, bf16[4,9,64,64]{3,2,1,0:T(8,128)(2,1)}, u32[]{:S(2)}) copy-start(bf16[4,9,64,64]{3,2,1,0:T(8,128)(2,1)} %param.10) | copy-start | bytes 884740
  1.3 9.2 %collective-permute-start = (bf16[2,64,512]{2,1,0:T(8,128)(2,1)S(1)}, bf16[2,64,512]{2,1,0:T(8,128)(2,1)S(1)}, u32[]{:S(2)}, u32[]{:S(2)}) collective-permute-start(bf16[2,64,512]{2,1,0:T(8,128)(2,1)S(1)} %slice.91), channel_id=1, source_target_pairs={{0,8},{8,16},{16,24},{24,32},{32,40},{40,48},{48,56},{56,64},{64,7... | collective-permute-start | bytes 393224 | tf_op jit(solution)/shard_map/ppermute | solution.py:17
  6.6 8.4 %collective-permute-start.1 = (bf16[2,64,512]{2,1,0:T(8,128)(2,1)S(1)}, bf16[2,64,512]{2,1,0:T(8,128)(2,1)S(1)}, u32[]{:S(2)}, u32[]{:S(2)}) collective-permute-start(bf16[2,64,512]{2,1,0:T(8,128)(2,1)S(1)} %slice.93), channel_id=1, source_target_pairs={{8,0},{16,8},{24,16},{32,24},{40,32},{48,40},{56,48},{64,56},{72,6... | collective-permute-start | bytes 393224 | tf_op jit(solution)/shard_map/ppermute | solution.py:20
  36.4 6.5 %copy-start.1 = (bf16[256,2,256]{2,1,0:T(2,128)(2,1)S(1)}, bf16[256,2,256]{2,1,0:T(2,128)(2,1)}, u32[]{:S(2)}) copy-start(bf16[256,2,256]{2,1,0:T(2,128)(2,1)} %param.9) | copy-start | bytes 786436
  38.6 5.9 %collective-permute-start.2 = (bf16[2,64,512]{2,1,0:T(8,128)(2,1)S(1)}, bf16[2,64,512]{2,1,0:T(8,128)(2,1)S(1)}, u32[]{:S(2)}, u32[]{:S(2)}) collective-permute-start(bf16[2,64,512]{2,1,0:T(8,128)(2,1)S(1)} %get-tuple-element.5), channel_id=1, source_target_pairs={{0,8},{8,16},{16,24},{24,32},{32,40},{40,48},{48,56},{56,64},{64,7... | collective-permute-start | bytes 393224 | tf_op jit(solution)/shard_map/ppermute | solution.py:17
  40.5 8.4 %collective-permute-start.3 = (bf16[2,64,512]{2,1,0:T(8,128)(2,1)S(1)}, bf16[2,64,512]{2,1,0:T(8,128)(2,1)S(1)}, u32[]{:S(2)}, u32[]{:S(2)}) collective-permute-start(bf16[2,64,512]{2,1,0:T(8,128)(2,1)S(1)} %get-tuple-element.6), channel_id=1, source_target_pairs={{8,0},{16,8},{24,16},{32,24},{40,32},{48,40},{56,48},{64,56},{72,6... | collective-permute-start | bytes 393224 | tf_op jit(solution)/shard_map/ppermute | solution.py:20
  56.2 1.1 %copy-start.3 = (bf16[4,64,512]{2,1,0:T(8,128)(2,1)S(1)}, bf16[4,64,512]{2,1,0:T(8,128)(2,1)}, u32[]{:S(2)}) copy-start(bf16[4,64,512]{2,1,0:T(8,128)(2,1)} %gather_fusion.11) | copy-start | bytes 786436
  56.4 1.1 %copy-start.4 = (bf16[4,64,512]{2,1,0:T(8,128)(2,1)S(1)}, bf16[4,64,512]{2,1,0:T(8,128)(2,1)}, u32[]{:S(2)}) copy-start(bf16[4,64,512]{2,1,0:T(8,128)(2,1)} %gather_fusion.10) | copy-start | bytes 786436
  56.7 1.1 %copy-start.5 = (bf16[4,64,512]{2,1,0:T(8,128)(2,1)S(1)}, bf16[4,64,512]{2,1,0:T(8,128)(2,1)}, u32[]{:S(2)}) copy-start(bf16[4,64,512]{2,1,0:T(8,128)(2,1)} %gather_fusion.17) | copy-start | bytes 786436
  57.9 1.0 copy-start.6
  57.9 1.0 %copy-start.7 = (bf16[512,256]{1,0:T(8,128)(2,1)S(1)}, bf16[512,256]{1,0:T(8,128)(2,1)}, u32[]{:S(2)}) copy-start(bf16[512,256]{1,0:T(8,128)(2,1)} %reshape.64) | copy-start | bytes 786436
  59.5 15.1 %copy-start.11 = (f32[256]{0:T(256)S(1)}, f32[256]{0:T(256)}, u32[]{:S(2)}) copy-start(f32[256]{0:T(256)} %param.13) | copy-start | bytes 3076
  73.0 1.8 %copy-start.8 = (bf16[256,256]{1,0:T(8,128)(2,1)S(1)}, bf16[256,256]{1,0:T(8,128)(2,1)}, u32[]{:S(2)}) copy-start(bf16[256,256]{1,0:T(8,128)(2,1)} %param.14) | copy-start | bytes 393220
  73.4 2.0 %copy-start.9 = (bf16[256,256]{1,0:T(8,128)(2,1)S(1)}, bf16[256,256]{1,0:T(8,128)(2,1)}, u32[]{:S(2)}) copy-start(bf16[256,256]{1,0:T(8,128)(2,1)} %param.15) | copy-start | bytes 393220
  83.7 1.0 %copy-start.10 = (bf16[256,256]{1,0:T(8,128)(2,1)S(1)}, bf16[256,256]{1,0:T(8,128)(2,1)}, u32[]{:S(2)}) copy-start(bf16[256,256]{1,0:T(8,128)(2,1)} %param.17) | copy-start | bytes 393220
